TPU v7x, 128 devices: a whole 4x4x4 slice. The times are simulated.
128 devices in a mesh: inner: 16 (over x_lo, z, core), outer: 8 (over x_hi, y).
Axes of the slice: x: 4 (x_hi: 2, x_lo: 2; x = x_hi * 2 + x_lo), y: 4, z: 4, core: 2. Of those that a mesh axis runs over, the one named last changes fastest.
Arguments:
- layer_input: bfloat16 [16384, 6144], P(('inner', 'outer')), may hold values from -0.25 to 0.25
- queries: bfloat16 [16384, 768], P(('inner', 'outer')), may hold values from -6 to 6
- keys_values: bfloat16 [16384, 256], P(('inner', 'outer')), may hold values from -6 to 6
- attn_out: bfloat16 [16384, 768], P(('inner', 'outer')), may hold values from -6 to 6
- out_grad: bfloat16 [16384, 768], P(('inner', 'outer')), may hold values from -6 to 6
- log_sums: float32 [6, 16384], P(None, ('inner', 'outer')), may hold values from 5 to 8
- doc_ids: int32 [16384], replicated, may hold values from 0 to 15, never falling along the last dimension, each value on 1 to 2048 neighbouring positions
- span_order: int32 [256], replicated, may hold values from 0 to 255, each once
Outputs:
- query_grad: bfloat16 [16384, 768], P(('inner', 'outer'))
- kv_grad: bfloat16 [16384, 256], P(('inner', 'outer'))
- weight_grad: float32 [6144, 256], P(('inner', 'outer'))
Inputs may be any that keep to these rules, and one draw needn't show every extreme that they name: `doc_ids`: never falling; each document holds 1 to 2048 positions. `span_order`: each span number once.
All inputs are finite; a program needn't handle non-finite values.
Results may differ from a plain program's by a relative error of at most 0.015.
Values may be sent and summed in bfloat16 or wider, within the bound.
A program may use at most 64 MiB of HBM per device.

v0:
```python
import jax
import jax.numpy as jnp
from jax import lax
from jax.sharding import PartitionSpec as P


def passed_along(value, axis, by):
    devices = lax.axis_size(axis)
    return lax.ppermute(value, axis, [(i, (i + by) % devices) for i in range(devices)])


def per_device(
    layer_input, queries, keys_values, attn_out, out_grad, log_sums, doc_ids, span_order
):
    tok_rows = keys_values.shape[0]
    half_len = tok_rows // 2
    head_count = log_sums.shape[0]
    head_dim = keys_values.shape[1] // 2
    inner_size = lax.axis_size("inner")
    outer_size = lax.axis_size("outer")
    my_index = lax.axis_index(("inner", "outer"))
    score_scale = head_dim ** (-0.5)
    row_ids = jnp.arange(tok_rows, dtype=jnp.int32)
    my_spans = lax.dynamic_slice_in_dim(span_order, 2 * my_index, 2)
    query_pos = (
        jnp.where(row_ids < half_len, my_spans[0], my_spans[1]) * half_len + row_ids % half_len
    )
    query_doc = jnp.take(doc_ids, query_pos)
    query_heads = queries.reshape(tok_rows, head_count, head_dim)
    grad_heads = out_grad.reshape(tok_rows, head_count, head_dim)
    out_heads = attn_out.reshape(tok_rows, head_count, head_dim)
    row_delta = jnp.einsum("ihc,ihc->hi", grad_heads, out_heads, preferred_element_type=jnp.float32)

    def key_meta(base_dev, stride, group_devs):
        key_ids = jnp.arange(group_devs * tok_rows, dtype=jnp.int32)
        owner = base_dev + key_ids // tok_rows * stride
        span_ids = 2 * owner + key_ids % tok_rows // half_len
        key_pos = jnp.take(span_order, span_ids) * half_len + key_ids % half_len
        return (key_pos, jnp.take(doc_ids, key_pos))

    def sweep(key_group, kv_grads, query_acc, key_pos, key_doc):
        group_len = key_group.shape[0]
        block_len = 512

        def one_block(block_idx, state):
            first = block_idx * block_len
            key_blk = lax.dynamic_slice_in_dim(key_group, first, block_len, 0)
            pos_blk = lax.dynamic_slice_in_dim(key_pos, first, block_len, 0)
            doc_blk = lax.dynamic_slice_in_dim(key_doc, first, block_len, 0)
            allowed = (pos_blk[None, :] <= query_pos[:, None]) & (
                doc_blk[None, :] == query_doc[:, None]
            )
            grads_now, query_now = state
            key_rows = key_blk[:, :head_dim]
            value_rows = key_blk[:, head_dim:]
            scores = (
                jnp.einsum("ihc,jc->hij", query_heads, key_rows, preferred_element_type=jnp.float32)
                * score_scale
            )
            probs = jnp.exp(jnp.where(allowed[None], scores - log_sums[:, :, None], -1e30))
            probs_low = probs.astype(jnp.bfloat16)
            prob_grads = jnp.einsum(
                "ihc,jc->hij", grad_heads, value_rows, preferred_element_type=jnp.float32
            )
            score_grads = (score_scale * probs * (prob_grads - row_delta[:, :, None])).astype(
                jnp.bfloat16
            )
            query_now = query_now + jnp.einsum(
                "hij,jc->ihc", score_grads, key_rows, preferred_element_type=jnp.float32
            )
            key_part = jnp.einsum(
                "hij,ihc->jc", score_grads, query_heads, preferred_element_type=jnp.float32
            )
            value_part = jnp.einsum(
                "hij,ihc->jc", probs_low, grad_heads, preferred_element_type=jnp.float32
            )
            updated = lax.dynamic_slice_in_dim(grads_now, first, block_len, 0) + jnp.concatenate(
                [key_part, value_part], axis=1
            )
            grads_now = lax.dynamic_update_slice_in_dim(grads_now, updated, first, 0)
            return (grads_now, query_now)

        return lax.fori_loop(0, group_len // block_len, one_block, (kv_grads, query_acc))

    query_zero = jnp.zeros((tok_rows, head_count, head_dim), jnp.float32)
    key_group = lax.all_gather(keys_values, "outer", axis=0, tiled=True)
    inner_pos = lax.axis_index("inner")

    def hop_inner(hop_idx, state):
        group_now, grads_now, query_now = state
        source = (inner_pos - hop_idx) % inner_size
        key_pos, key_doc = key_meta(source * outer_size, 1, outer_size)
        grads_now, query_now = sweep(group_now, grads_now, query_now, key_pos, key_doc)
        grads_now = passed_along(grads_now.astype(jnp.bfloat16), "inner", 1).astype(grads_now.dtype)
        group_now = passed_along(group_now, "inner", 1)
        return (group_now, grads_now, query_now)

    start = (key_group, jnp.zeros((key_group.shape[0], 2 * head_dim), jnp.float32), query_zero)
    key_group, kv_grads, query_acc = lax.fori_loop(0, inner_size, hop_inner, start)
    kv_total = lax.psum_scatter(
        kv_grads.astype(jnp.bfloat16), "outer", scatter_dimension=0, tiled=True
    )
    query_grad = query_acc.astype(jnp.bfloat16).reshape(tok_rows, head_count * head_dim)
    weight_grad = lax.psum_scatter(
        lax.dot_general(
            layer_input, kv_total, (((0,), (0,)), ((), ())), preferred_element_type=jnp.float32
        ),
        ("inner", "outer"),
        scatter_dimension=0,
        tiled=True,
    )
    return (query_grad, kv_total, weight_grad)


def solution(mesh):
    return jax.shard_map(
        per_device,
        mesh=mesh,
        in_specs=(
            P(("inner", "outer"), None),
            P(("inner", "outer"), None),
            P(("inner", "outer"), None),
            P(("inner", "outer"), None),
            P(("inner", "outer"), None),
            P(None, ("inner", "outer")),
            P(),
            P(),
        ),
        out_specs=(
            P(("inner", "outer"), None),
            P(("inner", "outer"), None),
            P(("inner", "outer"), None),
        ),
        check_vma=False,
    )
```

profile of v0, /device:TPU:0, one launch (start us, length us, event | category | flops | bytes accessed | tf_op | source)
XLA Modules:
  0.0 1487.1 jit_solution(5365712212598533073)
XLA Ops:
  16.5 35.7 %all_gather.3 = bf16[1024,256]{1,0:T(8,128)(2,1)S(1)} all-gather(bf16[128,256]{1,0:T(8,128)(2,1)S(1)} %copy-done.4), channel_id=1, replica_groups=mesh['inner'=16,'outer'=8] {'outer'}, dimensions={0}, use_global_device_ids=true | all-gather | bytes 589824 | tf_op jit(solution)/shard_map/all_gather | solution.py:86
  52.4 691.4 %while.64 = (s32[]{:T(128)}, bf16[1024,256]{1,0:T(8,128)(2,1)S(1)}, f32[1024,256]{0,1:T(8,128)}, f32[128,6,128]{0,2,1:T(8,128)S(1)}, s32[]{:T(128)}, /*index=5*/...) while((s32[]{:T(128)}, bf16[1024,256]{1,0:T(8,128)(2,1)S(1)}, ...), condition=%wide.region_3.4_spmd.clone, body=%wide.region_0.3_spmd.clone.sunk | while | flops 507945216 | bytes 26042736 | solution.py:99
  52.5 6.9 gather_fusion
  59.4 6.2 gather_fusion.1
  67.8 10.4 while.65
  81.1 8.9 collective-permute-done.1
  95.7 6.9 gather_fusion
  102.6 6.2 gather_fusion.1
  111.0 10.4 while.65
  122.3 10.9 collective-permute-done.1
  138.9 6.9 gather_fusion
  145.8 6.2 gather_fusion.1
  154.3 10.4 while.65
  165.5 10.9 collective-permute-done.1
  182.1 6.9 gather_fusion
  189.0 6.2 gather_fusion.1
  197.5 10.4 while.65
  208.7 10.9 collective-permute-done.1
  225.3 6.9 gather_fusion
  240.7 10.4 while.65
  251.9 10.9 collective-permute-done.1
  268.5 6.9 gather_fusion
  283.9 10.4 while.65
  295.1 10.9 collective-permute-done.1
  311.7 6.9 gather_fusion
  318.6 6.2 gather_fusion.1
  327.1 10.4 while.65
  338.3 10.9 collective-permute-done.1
  354.9 6.9 gather_fusion
  361.9 6.2 gather_fusion.1
  370.3 10.4 while.65
  381.6 10.9 collective-permute-done.1
  398.1 6.9 gather_fusion
  405.1 6.2 gather_fusion.1
  413.5 10.4 while.65
  424.8 10.9 collective-permute-done.1
  441.3 6.9 gather_fusion
  448.3 6.2 gather_fusion.1
  456.7 10.4 while.65
  468.0 10.9 collective-permute-done.1
  484.6 6.9 gather_fusion
  491.5 6.2 gather_fusion.1
  499.9 10.4 while.65
  511.2 10.9 collective-permute-done.1
  527.8 6.9 gather_fusion
  534.7 6.2 gather_fusion.1
  543.1 10.4 while.65
  554.4 10.9 collective-permute-done.1
  571.0 6.9 gather_fusion
  577.9 6.2 gather_fusion.1
  586.3 10.4 while.65
  597.6 10.9 collective-permute-done.1
  614.2 6.9 gather_fusion
  629.5 10.4 while.65
  640.8 10.9 collective-permute-done.1
  657.4 6.9 gather_fusion
  672.8 10.4 while.65
  684.0 10.9 collective-permute-done.1
  700.6 6.9 gather_fusion
  716.0 10.4 while.65
  727.2 10.9 collective-permute-done.1
  746.1 69.1 %reduce-scatter.5.cloned.1.call-done = bf16[128,256]{1,0:T(8,128)(2,1)} async-done(((bf16[1024,256]{1,0:T(8,128)(2,1)}), bf16[128,256]{1,0:T(8,128)(2,1)}) %reduce-scatter.5.cloned.1.call-update) | async-done | bytes 65552 | tf_op jit(solution)/shard_map/reduce_scatter | solution.py:100
  819.7 6.6 copy.62
  827.1 653.1 %reduce-scatter.7.cloned.1.call-done = f32[48,256]{1,0:T(8,128)} async-done(((f32[6144,256]{1,0:T(8,128)}), f32[48,256]{1,0:T(8,128)}) %reduce-scatter.7.cloned.1.call-update) | async-done | bytes 49168
  (563 shorter events, 354.5 us)
Async XLA Ops:
  7.2 808.0 %copy-start = (bf16[128,6144]{1,0:T(8,128)(2,1)S(1)}, bf16[128,6144]{1,0:T(8,128)(2,1)}, u32[]{:S(2)}) copy-start(bf16[128,6144]{1,0:T(8,128)(2,1)} %param.12) | copy-start | bytes 4718596
  7.2 45.2 %copy-start.1 = (s32[256]{0:T(256)S(1)}, s32[256]{0:T(256)}, u32[]{:S(2)}) copy-start(s32[256]{0:T(256)} %param.19) | copy-start | bytes 3076
  7.2 45.2 %copy-start.2 = (s32[16384]{0:T(1024)S(1)}, s32[16384]{0:T(1024)}, u32[]{:S(2)}) copy-start(s32[16384]{0:T(1024)} %param.18) | copy-start | bytes 196612
  7.2 9.3 copy-start.4
  7.2 45.2 %copy-start.5 = (f32[6,128]{1,0:T(8,128)S(1)}, f32[6,128]{1,0:T(8,128)}, u32[]{:S(2)}) copy-start(f32[6,128]{1,0:T(8,128)} %param.17) | copy-start | bytes 9220
  7.2 807.9 %reduce-scatter.5.cloned.1.call-start = ((), (), s32[]{:S(2)}) async-start(), calls=%async_computation.2 | async-start | bytes 589824 | tf_op jit(solution)/shard_map/reduce_scatter | solution.py:100
  65.6 2.2 copy-start.3
  79.1 10.9 collective-permute-start.1
  79.1 16.5 %collective-permute-start = (bf16[1024,256]{1,0:T(8,128)(2,1)}, bf16[1024,256]{1,0:T(8,128)(2,1)S(1)}, u32[]{:S(2)}, u32[]{:S(2)}) collective-permute-start(bf16[1024,256]{1,0:T(8,128)(2,1)} %copy.80), channel_id=1, source_target_pairs={{0,8},{8,16},{16,24},{24,32},{32,40},{40,48},{48,56},{56,64},{64,7... | collective-permute-start | bytes 1572872 | tf_op jit(solution)/shard_map/while/body/eval_jaxpr/ppermute | solution.py:9
  108.8 2.2 copy-start.3
  122.3 10.9 collective-permute-start.1
  122.3 16.5 %collective-permute-start = (bf16[1024,256]{1,0:T(8,128)(2,1)}, bf16[1024,256]{1,0:T(8,128)(2,1)S(1)}, u32[]{:S(2)}, u32[]{:S(2)}) collective-permute-start(bf16[1024,256]{1,0:T(8,128)(2,1)} %copy.80), channel_id=1, source_target_pairs={{0,8},{8,16},{16,24},{24,32},{32,40},{40,48},{48,56},{56,64},{64,7... | collective-permute-start | bytes 1572872 | tf_op jit(solution)/shard_map/while/body/eval_jaxpr/ppermute | solution.py:9
  152.0 2.2 copy-start.3
  165.5 10.9 collective-permute-start.1
  165.5 16.5 %collective-permute-start = (bf16[1024,256]{1,0:T(8,128)(2,1)}, bf16[1024,256]{1,0:T(8,128)(2,1)S(1)}, u32[]{:S(2)}, u32[]{:S(2)}) collective-permute-start(bf16[1024,256]{1,0:T(8,128)(2,1)} %copy.80), channel_id=1, source_target_pairs={{0,8},{8,16},{16,24},{24,32},{32,40},{40,48},{48,56},{56,64},{64,7... | collective-permute-start | bytes 1572872 | tf_op jit(solution)/shard_map/while/body/eval_jaxpr/ppermute | solution.py:9
  195.2 2.2 copy-start.3
  208.7 10.9 collective-permute-start.1
  208.7 16.5 %collective-permute-start = (bf16[1024,256]{1,0:T(8,128)(2,1)}, bf16[1024,256]{1,0:T(8,128)(2,1)S(1)}, u32[]{:S(2)}, u32[]{:S(2)}) collective-permute-start(bf16[1024,256]{1,0:T(8,128)(2,1)} %copy.80), channel_id=1, source_target_pairs={{0,8},{8,16},{16,24},{24,32},{32,40},{40,48},{48,56},{56,64},{64,7... | collective-permute-start | bytes 1572872 | tf_op jit(solution)/shard_map/while/body/eval_jaxpr/ppermute | solution.py:9
  238.4 2.2 copy-start.3
  251.9 10.9 collective-permute-start.1
  251.9 16.5 %collective-permute-start = (bf16[1024,256]{1,0:T(8,128)(2,1)}, bf16[1024,256]{1,0:T(8,128)(2,1)S(1)}, u32[]{:S(2)}, u32[]{:S(2)}) collective-permute-start(bf16[1024,256]{1,0:T(8,128)(2,1)} %copy.80), channel_id=1, source_target_pairs={{0,8},{8,16},{16,24},{24,32},{32,40},{40,48},{48,56},{56,64},{64,7... | collective-permute-start | bytes 1572872 | tf_op jit(solution)/shard_map/while/body/eval_jaxpr/ppermute | solution.py:9
  281.6 2.2 copy-start.3
  295.1 10.9 collective-permute-start.1
  295.1 16.5 %collective-permute-start = (bf16[1024,256]{1,0:T(8,128)(2,1)}, bf16[1024,256]{1,0:T(8,128)(2,1)S(1)}, u32[]{:S(2)}, u32[]{:S(2)}) collective-permute-start(bf16[1024,256]{1,0:T(8,128)(2,1)} %copy.80), channel_id=1, source_target_pairs={{0,8},{8,16},{16,24},{24,32},{32,40},{40,48},{48,56},{56,64},{64,7... | collective-permute-start | bytes 1572872 | tf_op jit(solution)/shard_map/while/body/eval_jaxpr/ppermute | solution.py:9
  324.8 2.2 copy-start.3
  338.3 10.9 collective-permute-start.1
  338.3 16.5 %collective-permute-start = (bf16[1024,256]{1,0:T(8,128)(2,1)}, bf16[1024,256]{1,0:T(8,128)(2,1)S(1)}, u32[]{:S(2)}, u32[]{:S(2)}) collective-permute-start(bf16[1024,256]{1,0:T(8,128)(2,1)} %copy.80), channel_id=1, source_target_pairs={{0,8},{8,16},{16,24},{24,32},{32,40},{40,48},{48,56},{56,64},{64,7... | collective-permute-start | bytes 1572872 | tf_op jit(solution)/shard_map/while/body/eval_jaxpr/ppermute | solution.py:9
  368.0 2.2 copy-start.3
  381.5 10.9 collective-permute-start.1
  381.6 16.5 %collective-permute-start = (bf16[1024,256]{1,0:T(8,128)(2,1)}, bf16[1024,256]{1,0:T(8,128)(2,1)S(1)}, u32[]{:S(2)}, u32[]{:S(2)}) collective-permute-start(bf16[1024,256]{1,0:T(8,128)(2,1)} %copy.80), channel_id=1, source_target_pairs={{0,8},{8,16},{16,24},{24,32},{32,40},{40,48},{48,56},{56,64},{64,7... | collective-permute-start | bytes 1572872 | tf_op jit(solution)/shard_map/while/body/eval_jaxpr/ppermute | solution.py:9
  411.2 2.2 copy-start.3
  424.8 10.9 collective-permute-start.1
  424.8 16.5 %collective-permute-start = (bf16[1024,256]{1,0:T(8,128)(2,1)}, bf16[1024,256]{1,0:T(8,128)(2,1)S(1)}, u32[]{:S(2)}, u32[]{:S(2)}) collective-permute-start(bf16[1024,256]{1,0:T(8,128)(2,1)} %copy.80), channel_id=1, source_target_pairs={{0,8},{8,16},{16,24},{24,32},{32,40},{40,48},{48,56},{56,64},{64,7... | collective-permute-start | bytes 1572872 | tf_op jit(solution)/shard_map/while/body/eval_jaxpr/ppermute | solution.py:9
  454.4 2.2 copy-start.3
  468.0 10.9 collective-permute-start.1
  468.0 16.5 %collective-permute-start = (bf16[1024,256]{1,0:T(8,128)(2,1)}, bf16[1024,256]{1,0:T(8,128)(2,1)S(1)}, u32[]{:S(2)}, u32[]{:S(2)}) collective-permute-start(bf16[1024,256]{1,0:T(8,128)(2,1)} %copy.80), channel_id=1, source_target_pairs={{0,8},{8,16},{16,24},{24,32},{32,40},{40,48},{48,56},{56,64},{64,7... | collective-permute-start | bytes 1572872 | tf_op jit(solution)/shard_map/while/body/eval_jaxpr/ppermute | solution.py:9
  497.6 2.2 copy-start.3
  511.2 10.9 collective-permute-start.1
  511.2 16.5 %collective-permute-start = (bf16[1024,256]{1,0:T(8,128)(2,1)}, bf16[1024,256]{1,0:T(8,128)(2,1)S(1)}, u32[]{:S(2)}, u32[]{:S(2)}) collective-permute-start(bf16[1024,256]{1,0:T(8,128)(2,1)} %copy.80), channel_id=1, source_target_pairs={{0,8},{8,16},{16,24},{24,32},{32,40},{40,48},{48,56},{56,64},{64,7... | collective-permute-start | bytes 1572872 | tf_op jit(solution)/shard_map/while/body/eval_jaxpr/ppermute | solution.py:9
  540.8 2.2 copy-start.3
  554.4 10.9 collective-permute-start.1
  554.4 16.5 %collective-permute-start = (bf16[1024,256]{1,0:T(8,128)(2,1)}, bf16[1024,256]{1,0:T(8,128)(2,1)S(1)}, u32[]{:S(2)}, u32[]{:S(2)}) collective-permute-start(bf16[1024,256]{1,0:T(8,128)(2,1)} %copy.80), channel_id=1, source_target_pairs={{0,8},{8,16},{16,24},{24,32},{32,40},{40,48},{48,56},{56,64},{64,7... | collective-permute-start | bytes 1572872 | tf_op jit(solution)/shard_map/while/body/eval_jaxpr/ppermute | solution.py:9
  584.1 2.2 copy-start.3
  597.6 10.9 collective-permute-start.1
  597.6 16.5 %collective-permute-start = (bf16[1024,256]{1,0:T(8,128)(2,1)}, bf16[1024,256]{1,0:T(8,128)(2,1)S(1)}, u32[]{:S(2)}, u32[]{:S(2)}) collective-permute-start(bf16[1024,256]{1,0:T(8,128)(2,1)} %copy.80), channel_id=1, source_target_pairs={{0,8},{8,16},{16,24},{24,32},{32,40},{40,48},{48,56},{56,64},{64,7... | collective-permute-start | bytes 1572872 | tf_op jit(solution)/shard_map/while/body/eval_jaxpr/ppermute | solution.py:9
  627.3 2.2 copy-start.3
  640.8 10.9 collective-permute-start.1
  640.8 16.5 %collective-permute-start = (bf16[1024,256]{1,0:T(8,128)(2,1)}, bf16[1024,256]{1,0:T(8,128)(2,1)S(1)}, u32[]{:S(2)}, u32[]{:S(2)}) collective-permute-start(bf16[1024,256]{1,0:T(8,128)(2,1)} %copy.80), channel_id=1, source_target_pairs={{0,8},{8,16},{16,24},{24,32},{32,40},{40,48},{48,56},{56,64},{64,7... | collective-permute-start | bytes 1572872 | tf_op jit(solution)/shard_map/while/body/eval_jaxpr/ppermute | solution.py:9
  670.5 2.2 copy-start.3
  684.0 10.9 collective-permute-start.1
  684.0 16.5 %collective-permute-start = (bf16[1024,256]{1,0:T(8,128)(2,1)}, bf16[1024,256]{1,0:T(8,128)(2,1)S(1)}, u32[]{:S(2)}, u32[]{:S(2)}) collective-permute-start(bf16[1024,256]{1,0:T(8,128)(2,1)} %copy.80), channel_id=1, source_target_pairs={{0,8},{8,16},{16,24},{24,32},{32,40},{40,48},{48,56},{56,64},{64,7... | collective-permute-start | bytes 1572872 | tf_op jit(solution)/shard_map/while/body/eval_jaxpr/ppermute | solution.py:9
  713.7 2.2 copy-start.3
  727.2 10.9 collective-permute-start.1
  727.2 16.5 %collective-permute-start = (bf16[1024,256]{1,0:T(8,128)(2,1)}, bf16[1024,256]{1,0:T(8,128)(2,1)S(1)}, u32[]{:S(2)}, u32[]{:S(2)}) collective-permute-start(bf16[1024,256]{1,0:T(8,128)(2,1)} %copy.80), channel_id=1, source_target_pairs={{0,8},{8,16},{16,24},{24,32},{32,40},{40,48},{48,56},{56,64},{64,7... | collective-permute-start | bytes 1572872 | tf_op jit(solution)/shard_map/while/body/eval_jaxpr/ppermute | solution.py:9
  746.0 734.2 %reduce-scatter.7.cloned.1.call-start = ((), (), s32[]{:S(2)}) async-start(), calls=%async_computation.3 | async-start | bytes 6340608
Sparse Core Ops, SparseCore 0:
  746.2 68.9 reduce-scatter.4
  826.4 653.8 reduce-scatter.6
where the time goes:
time: 1490 us
  waiting for transfers between devices  968 us (65%)
  local copies, waits for them, and re-layouts  243 us (16%)
  matrix products  153 us (10%)
  other arithmetic  68.1 us (5%)
  blocking collectives  35.7 us (2%)
    unnamed x3, waiting for transfers between devices  653 us
    ppermute x32, waiting for transfers between devices, passed_along(): lax.ppermute(value, axis, [(i, (i + by) % devices) for i in range(devices)])  245 us
    gather x16, local copies, waits for them, and re-layouts, key_meta(): key_pos = jnp.take(span_order, span_ids) * half_len + key_ids % half_len  110 us
    gather x16, local copies, waits for them, and re-layouts, key_meta(): return (key_pos, jnp.take(doc_ids, key_pos))  98.5 us
    reduce_scatter x1, waiting for transfers between devices, per_device(): lax.psum_scatter(kv_grads.astype(jnp.bfloat16), 'outer', scatter_dimensio...  69.1 us
    dot_general x32, matrix products, one_block(): jnp.einsum('ihc,jc->hij', query_heads, key_rows, preferred_element_type=j...  43.8 us
    dot_general x32, matrix products, one_block(): jnp.einsum('ihc,jc->hij', grad_heads, value_rows, preferred_element_type=...  41 us
    dot_general x32, matrix products, one_block(): jnp.einsum('hij,jc->ihc', score_grads, key_rows, preferred_element_type=j...  39 us
  transfers between devices with their start and end apart: 34, of which 34 were waited for; matrix products, arithmetic and copies ran while one was open for 1% of the time, Pallas kernels for 0%

commit v1 on v0

--- a/solution.py
+++ b/solution.py
@@ -83,7 +83,9 @@
         return lax.fori_loop(0, group_len // block_len, one_block, (kv_grads, query_acc))
 
     query_zero = jnp.zeros((tok_rows, head_count, head_dim), jnp.float32)
-    key_group = lax.all_gather(keys_values, "outer", axis=0, tiled=True)
+    key_group = jnp.concatenate(
+        lax.all_to_all(jnp.stack([keys_values] * lax.axis_size("outer")), "outer", 0, 0), axis=0
+    )
     inner_pos = lax.axis_index("inner")
 
     def hop_inner(hop_idx, state):

time: 1490 us -> 1460 us (0.980)
  blocking collectives: 35.7 us -> 0 us
    all_gather x1 -> x0, blocking collectives: 35.7 us -> none  [per_device(): key_group = lax.all_gather(keys_values, 'outer', axis=0, tiled=True)]
  transfers between devices with their start and end apart: 34 -> 35, of which waited for: 34 -> 35; matrix products, arithmetic and copies ran while one was open for 1% -> 2% of each run, Pallas kernels for 0% -> 0%
where the time goes in v1:
time: 1460 us
  waiting for transfers between devices  971 us (67%)
  local copies, waits for them, and re-layouts  240 us (16%)
  matrix products  153 us (10%)
  other arithmetic  69.1 us (5%)
    unnamed x3, waiting for transfers between devices  653 us
    ppermute x32, waiting for transfers between devices, passed_along(): lax.ppermute(value, axis, [(i, (i + by) % devices) for i in range(devices)])  245 us
    gather x16, local copies, waits for them, and re-layouts, key_meta(): key_pos = jnp.take(span_order, span_ids) * half_len + key_ids % half_len  110 us
    gather x16, local copies, waits for them, and re-layouts, key_meta(): return (key_pos, jnp.take(doc_ids, key_pos))  98.5 us
    reduce_scatter x1, waiting for transfers between devices, per_device(): lax.psum_scatter(kv_grads.astype(jnp.bfloat16), 'outer', scatter_dimensio...  66.8 us
    dot_general x32, matrix products, one_block(): jnp.einsum('ihc,jc->hij', query_heads, key_rows, preferred_element_type=j...  43.8 us
    dot_general x32, matrix products, one_block(): jnp.einsum('ihc,jc->hij', grad_heads, value_rows, preferred_element_type=...  41 us
    dot_general x32, matrix products, one_block(): jnp.einsum('hij,jc->ihc', score_grads, key_rows, preferred_element_type=j...  39 us
  transfers between devices with their start and end apart: 35, of which 35 were waited for; matrix products, arithmetic and copies ran while one was open for 2% of the time, Pallas kernels for 0%

profile of v1, /device:TPU:0, one launch (start us, length us, event | category | flops | bytes accessed | tf_op | source)
XLA Modules:
  0.0 1460.5 jit_solution(4468271606501329182)
XLA Ops:
  9.1 7.2 all-to-all-start
  27.3 692.3 %while.64 = (s32[]{:T(128)}, bf16[1024,256]{1,0:T(8,128)(2,1)S(1)}, f32[1024,256]{0,1:T(8,128)}, f32[128,6,128]{0,2,1:T(8,128)S(1)}, s32[]{:T(128)}, /*index=5*/...) while((s32[]{:T(128)}, bf16[1024,256]{1,0:T(8,128)(2,1)S(1)}, ...), condition=%wide.region_3.4_spmd.clone, body=%wide.region_0.3_spmd.clone.sunk | while | flops 507945216 | bytes 26042736 | solution.py:101
  27.4 6.9 gather_fusion
  34.3 6.2 gather_fusion.1
  42.8 10.4 while.65
  56.1 8.9 collective-permute-done.1
  70.7 6.9 gather_fusion
  77.6 6.2 gather_fusion.1
  86.1 10.4 while.65
  97.4 10.9 collective-permute-done.1
  113.9 6.9 gather_fusion
  120.9 6.2 gather_fusion.1
  129.4 10.4 while.65
  140.6 10.9 collective-permute-done.1
  157.2 6.9 gather_fusion
  164.1 6.2 gather_fusion.1
  172.6 10.4 while.65
  183.9 10.9 collective-permute-done.1
  200.5 6.9 gather_fusion
  207.4 6.2 gather_fusion.1
  215.9 10.4 while.65
  227.2 10.9 collective-permute-done.1
  243.8 6.9 gather_fusion
  259.2 10.4 while.65
  270.4 10.9 collective-permute-done.1
  287.0 6.9 gather_fusion
  293.9 6.2 gather_fusion.1
  302.4 10.4 while.65
  313.7 10.9 collective-permute-done.1
  330.3 6.9 gather_fusion
  337.2 6.2 gather_fusion.1
  345.7 10.4 while.65
  357.0 10.9 collective-permute-done.1
  373.6 6.9 gather_fusion
  380.5 6.2 gather_fusion.1
  389.0 10.4 while.65
  400.2 10.9 collective-permute-done.1
  416.8 6.9 gather_fusion
  423.7 6.2 gather_fusion.1
  432.2 10.4 while.65
  443.5 10.9 collective-permute-done.1
  460.1 6.9 gather_fusion
  467.0 6.2 gather_fusion.1
  475.5 10.4 while.65
  486.8 10.9 collective-permute-done.1
  503.4 6.9 gather_fusion
  510.3 6.2 gather_fusion.1
  518.8 10.4 while.65
  530.0 10.9 collective-permute-done.1
  546.6 6.9 gather_fusion
  562.1 10.4 while.65
  573.3 10.9 collective-permute-done.1
  589.9 6.9 gather_fusion
  605.3 10.4 while.65
  616.6 10.9 collective-permute-done.1
  633.2 6.9 gather_fusion
  648.6 10.4 while.65
  659.8 10.9 collective-permute-done.1
  676.4 6.9 gather_fusion
  691.9 10.4 while.65
  703.1 10.9 collective-permute-done.1
  722.0 66.8 %reduce-scatter.5.cloned.1.call-done = bf16[128,256]{1,0:T(8,128)(2,1)} async-done(((bf16[1024,256]{1,0:T(8,128)(2,1)}), bf16[128,256]{1,0:T(8,128)(2,1)}) %reduce-scatter.5.cloned.1.call-update) | async-done | bytes 65552 | tf_op jit(solution)/shard_map/reduce_scatter | solution.py:102
  793.3 6.6 copy.62
  800.7 652.9 %reduce-scatter.7.cloned.1.call-done = f32[48,256]{1,0:T(8,128)} async-done(((f32[6144,256]{1,0:T(8,128)}), f32[48,256]{1,0:T(8,128)}) %reduce-scatter.7.cloned.1.call-update) | async-done | bytes 49168
  (569 shorter events, 358.9 us)
Async XLA Ops:
  7.2 781.6 %copy-start = (bf16[128,6144]{1,0:T(8,128)(2,1)S(1)}, bf16[128,6144]{1,0:T(8,128)(2,1)}, u32[]{:S(2)}) copy-start(bf16[128,6144]{1,0:T(8,128)(2,1)} %param.12) | copy-start | bytes 4718596
  7.2 9.1 copy-start.1
  7.2 9.9 copy-start.4
  7.2 10.0 copy-start.5
  7.2 10.2 copy-start.6
  7.2 11.7 copy-start.2
  9.1 18.2 %copy-start.7 = (f32[6,128]{1,0:T(8,128)S(1)}, f32[6,128]{1,0:T(8,128)}, u32[]{:S(2)}) copy-start(f32[6,128]{1,0:T(8,128)} %param.17) | copy-start | bytes 9220
  9.1 18.2 %all-to-all-start = ((bf16[8,128,256]{2,1,0:T(8,128)(2,1)}), bf16[8,128,256]{2,1,0:T(8,128)(2,1)S(1)}, u32[]{:S(2)}, u32[]{:S(2)}) async-start(bf16[8,128,256]{2,1,0:T(8,128)(2,1)} %stack.2), calls=%async_computation | async-start | bytes 1048576 | tf_op jit(solution)/shard_map/all_to_all | solution.py:87
  16.3 772.5 %reduce-scatter.5.cloned.1.call-start = ((), (), s32[]{:S(2)}) async-start(), calls=%async_computation.3 | async-start | bytes 589824 | tf_op jit(solution)/shard_map/reduce_scatter | solution.py:102
  40.5 2.2 copy-start.3
  54.1 10.9 collective-permute-start.1
  54.1 16.5 %collective-permute-start = (bf16[1024,256]{1,0:T(8,128)(2,1)}, bf16[1024,256]{1,0:T(8,128)(2,1)S(1)}, u32[]{:S(2)}, u32[]{:S(2)}) collective-permute-start(bf16[1024,256]{1,0:T(8,128)(2,1)} %copy.80), channel_id=1, source_target_pairs={{0,8},{8,16},{16,24},{24,32},{32,40},{40,48},{48,56},{56,64},{64,7... | collective-permute-start | bytes 1572872 | tf_op jit(solution)/shard_map/while/body/eval_jaxpr/ppermute | solution.py:9
  83.8 2.2 copy-start.3
  97.4 10.9 collective-permute-start.1
  97.4 16.5 %collective-permute-start = (bf16[1024,256]{1,0:T(8,128)(2,1)}, bf16[1024,256]{1,0:T(8,128)(2,1)S(1)}, u32[]{:S(2)}, u32[]{:S(2)}) collective-permute-start(bf16[1024,256]{1,0:T(8,128)(2,1)} %copy.80), channel_id=1, source_target_pairs={{0,8},{8,16},{16,24},{24,32},{32,40},{40,48},{48,56},{56,64},{64,7... | collective-permute-start | bytes 1572872 | tf_op jit(solution)/shard_map/while/body/eval_jaxpr/ppermute | solution.py:9
  127.0 2.2 copy-start.3
  140.6 10.9 collective-permute-start.1
  140.6 16.5 %collective-permute-start = (bf16[1024,256]{1,0:T(8,128)(2,1)}, bf16[1024,256]{1,0:T(8,128)(2,1)S(1)}, u32[]{:S(2)}, u32[]{:S(2)}) collective-permute-start(bf16[1024,256]{1,0:T(8,128)(2,1)} %copy.80), channel_id=1, source_target_pairs={{0,8},{8,16},{16,24},{24,32},{32,40},{40,48},{48,56},{56,64},{64,7... | collective-permute-start | bytes 1572872 | tf_op jit(solution)/shard_map/while/body/eval_jaxpr/ppermute | solution.py:9
  170.3 2.2 copy-start.3
  183.9 10.9 collective-permute-start.1
  183.9 16.5 %collective-permute-start = (bf16[1024,256]{1,0:T(8,128)(2,1)}, bf16[1024,256]{1,0:T(8,128)(2,1)S(1)}, u32[]{:S(2)}, u32[]{:S(2)}) collective-permute-start(bf16[1024,256]{1,0:T(8,128)(2,1)} %copy.80), channel_id=1, source_target_pairs={{0,8},{8,16},{16,24},{24,32},{32,40},{40,48},{48,56},{56,64},{64,7... | collective-permute-start | bytes 1572872 | tf_op jit(solution)/shard_map/while/body/eval_jaxpr/ppermute | solution.py:9
  213.6 2.2 copy-start.3
  227.2 10.9 collective-permute-start.1
  227.2 16.5 %collective-permute-start = (bf16[1024,256]{1,0:T(8,128)(2,1)}, bf16[1024,256]{1,0:T(8,128)(2,1)S(1)}, u32[]{:S(2)}, u32[]{:S(2)}) collective-permute-start(bf16[1024,256]{1,0:T(8,128)(2,1)} %copy.80), channel_id=1, source_target_pairs={{0,8},{8,16},{16,24},{24,32},{32,40},{40,48},{48,56},{56,64},{64,7... | collective-permute-start | bytes 1572872 | tf_op jit(solution)/shard_map/while/body/eval_jaxpr/ppermute | solution.py:9
  256.8 2.2 copy-start.3
  270.4 10.9 collective-permute-start.1
  270.4 16.5 %collective-permute-start = (bf16[1024,256]{1,0:T(8,128)(2,1)}, bf16[1024,256]{1,0:T(8,128)(2,1)S(1)}, u32[]{:S(2)}, u32[]{:S(2)}) collective-permute-start(bf16[1024,256]{1,0:T(8,128)(2,1)} %copy.80), channel_id=1, source_target_pairs={{0,8},{8,16},{16,24},{24,32},{32,40},{40,48},{48,56},{56,64},{64,7... | collective-permute-start | bytes 1572872 | tf_op jit(solution)/shard_map/while/body/eval_jaxpr/ppermute | solution.py:9
  300.1 2.2 copy-start.3
  313.7 10.9 collective-permute-start.1
  313.7 16.5 %collective-permute-start = (bf16[1024,256]{1,0:T(8,128)(2,1)}, bf16[1024,256]{1,0:T(8,128)(2,1)S(1)}, u32[]{:S(2)}, u32[]{:S(2)}) collective-permute-start(bf16[1024,256]{1,0:T(8,128)(2,1)} %copy.80), channel_id=1, source_target_pairs={{0,8},{8,16},{16,24},{24,32},{32,40},{40,48},{48,56},{56,64},{64,7... | collective-permute-start | bytes 1572872 | tf_op jit(solution)/shard_map/while/body/eval_jaxpr/ppermute | solution.py:9
  343.4 2.2 copy-start.3
  357.0 10.9 collective-permute-start.1
  357.0 16.5 %collective-permute-start = (bf16[1024,256]{1,0:T(8,128)(2,1)}, bf16[1024,256]{1,0:T(8,128)(2,1)S(1)}, u32[]{:S(2)}, u32[]{:S(2)}) collective-permute-start(bf16[1024,256]{1,0:T(8,128)(2,1)} %copy.80), channel_id=1, source_target_pairs={{0,8},{8,16},{16,24},{24,32},{32,40},{40,48},{48,56},{56,64},{64,7... | collective-permute-start | bytes 1572872 | tf_op jit(solution)/shard_map/while/body/eval_jaxpr/ppermute | solution.py:9
  386.6 2.2 copy-start.3
  400.2 10.9 collective-permute-start.1
  400.2 16.5 %collective-permute-start = (bf16[1024,256]{1,0:T(8,128)(2,1)}, bf16[1024,256]{1,0:T(8,128)(2,1)S(1)}, u32[]{:S(2)}, u32[]{:S(2)}) collective-permute-start(bf16[1024,256]{1,0:T(8,128)(2,1)} %copy.80), channel_id=1, source_target_pairs={{0,8},{8,16},{16,24},{24,32},{32,40},{40,48},{48,56},{56,64},{64,7... | collective-permute-start | bytes 1572872 | tf_op jit(solution)/shard_map/while/body/eval_jaxpr/ppermute | solution.py:9
  429.9 2.2 copy-start.3
  443.5 10.9 collective-permute-start.1
  443.5 16.5 %collective-permute-start = (bf16[1024,256]{1,0:T(8,128)(2,1)}, bf16[1024,256]{1,0:T(8,128)(2,1)S(1)}, u32[]{:S(2)}, u32[]{:S(2)}) collective-permute-start(bf16[1024,256]{1,0:T(8,128)(2,1)} %copy.80), channel_id=1, source_target_pairs={{0,8},{8,16},{16,24},{24,32},{32,40},{40,48},{48,56},{56,64},{64,7... | collective-permute-start | bytes 1572872 | tf_op jit(solution)/shard_map/while/body/eval_jaxpr/ppermute | solution.py:9
  473.2 2.2 copy-start.3
  486.8 10.9 collective-permute-start.1
  486.8 16.5 %collective-permute-start = (bf16[1024,256]{1,0:T(8,128)(2,1)}, bf16[1024,256]{1,0:T(8,128)(2,1)S(1)}, u32[]{:S(2)}, u32[]{:S(2)}) collective-permute-start(bf16[1024,256]{1,0:T(8,128)(2,1)} %copy.80), channel_id=1, source_target_pairs={{0,8},{8,16},{16,24},{24,32},{32,40},{40,48},{48,56},{56,64},{64,7... | collective-permute-start | bytes 1572872 | tf_op jit(solution)/shard_map/while/body/eval_jaxpr/ppermute | solution.py:9
  516.4 2.2 copy-start.3
  530.0 10.9 collective-permute-start.1
  530.0 16.5 %collective-permute-start = (bf16[1024,256]{1,0:T(8,128)(2,1)}, bf16[1024,256]{1,0:T(8,128)(2,1)S(1)}, u32[]{:S(2)}, u32[]{:S(2)}) collective-permute-start(bf16[1024,256]{1,0:T(8,128)(2,1)} %copy.80), channel_id=1, source_target_pairs={{0,8},{8,16},{16,24},{24,32},{32,40},{40,48},{48,56},{56,64},{64,7... | collective-permute-start | bytes 1572872 | tf_op jit(solution)/shard_map/while/body/eval_jaxpr/ppermute | solution.py:9
  559.7 2.2 copy-start.3
  573.3 10.9 collective-permute-start.1
  573.3 16.5 %collective-permute-start = (bf16[1024,256]{1,0:T(8,128)(2,1)}, bf16[1024,256]{1,0:T(8,128)(2,1)S(1)}, u32[]{:S(2)}, u32[]{:S(2)}) collective-permute-start(bf16[1024,256]{1,0:T(8,128)(2,1)} %copy.80), channel_id=1, source_target_pairs={{0,8},{8,16},{16,24},{24,32},{32,40},{40,48},{48,56},{56,64},{64,7... | collective-permute-start | bytes 1572872 | tf_op jit(solution)/shard_map/while/body/eval_jaxpr/ppermute | solution.py:9
  603.0 2.2 copy-start.3
  616.6 10.9 collective-permute-start.1
  616.6 16.5 %collective-permute-start = (bf16[1024,256]{1,0:T(8,128)(2,1)}, bf16[1024,256]{1,0:T(8,128)(2,1)S(1)}, u32[]{:S(2)}, u32[]{:S(2)}) collective-permute-start(bf16[1024,256]{1,0:T(8,128)(2,1)} %copy.80), channel_id=1, source_target_pairs={{0,8},{8,16},{16,24},{24,32},{32,40},{40,48},{48,56},{56,64},{64,7... | collective-permute-start | bytes 1572872 | tf_op jit(solution)/shard_map/while/body/eval_jaxpr/ppermute | solution.py:9
  646.2 2.2 copy-start.3
  659.8 10.9 collective-permute-start.1
  659.8 16.5 %collective-permute-start = (bf16[1024,256]{1,0:T(8,128)(2,1)}, bf16[1024,256]{1,0:T(8,128)(2,1)S(1)}, u32[]{:S(2)}, u32[]{:S(2)}) collective-permute-start(bf16[1024,256]{1,0:T(8,128)(2,1)} %copy.80), channel_id=1, source_target_pairs={{0,8},{8,16},{16,24},{24,32},{32,40},{40,48},{48,56},{56,64},{64,7... | collective-permute-start | bytes 1572872 | tf_op jit(solution)/shard_map/while/body/eval_jaxpr/ppermute | solution.py:9
  689.5 2.2 copy-start.3
  703.1 10.9 collective-permute-start.1
  703.1 16.5 %collective-permute-start = (bf16[1024,256]{1,0:T(8,128)(2,1)}, bf16[1024,256]{1,0:T(8,128)(2,1)S(1)}, u32[]{:S(2)}, u32[]{:S(2)}) collective-permute-start(bf16[1024,256]{1,0:T(8,128)(2,1)} %copy.80), channel_id=1, source_target_pairs={{0,8},{8,16},{16,24},{24,32},{32,40},{40,48},{48,56},{56,64},{64,7... | collective-permute-start | bytes 1572872 | tf_op jit(solution)/shard_map/while/body/eval_jaxpr/ppermute | solution.py:9
  721.9 731.7 %reduce-scatter.7.cloned.1.call-start = ((), (), s32[]{:S(2)}) async-start(), calls=%async_computation.4 | async-start | bytes 6340608
Sparse Core Ops, SparseCore 0:
  722.1 66.6 reduce-scatter.4
  800.0 653.6 reduce-scatter.6
